TPU v7x, 256 devices: a whole 4x4x8 slice. The times are simulated.
256 devices in a mesh: aux: 8 (over x, core), orb: 32 (over z, y).
Axes of the slice: x: 4, y: 4, z: 8, core: 2. Of those that a mesh axis runs over, the one named last changes fastest.
Arguments:
- three_center: float32 [32, 32, 128, 1024], P('aux', 'orb'), may hold values from -6 to 6
- tile_lists: int32 [2, 32, 8, 8], P(None, 'aux'), may hold values from -1 to 7, as said below
- occ_density: float32 [2, 1024, 1024], P(None, 'orb', 'aux'), may hold values from -0.1875 to 0.1875
- vir_density: float32 [2, 1024, 1024], P(None, 'orb', 'aux'), may hold values from -0.1875 to 0.1875
Outputs:
- coupled: float32 [2, 32, 32, 1024, 128], P(None, 'aux', 'orb')
Inputs may be any that keep to these rules, and one draw needn't show every extreme that they name: Row m of tile_lists[t, j] names distinct orbital blocks in rising order, block m always among them, and -1 in the remaining places; it names between 2 and 8 blocks, and for every t and j one row names all 8 and another exactly 2.
All inputs are finite; a program needn't handle non-finite values.
Results may differ from a plain program's by a relative error of at most 0.0003.
Values sent between devices are 32-bit elements; how exact they have to be, the bound alone decides.
A program may use at most 64 MiB of HBM per device.

v0:
```python
import jax
import jax.numpy as jnp
from jax import lax
from jax.sharding import PartitionSpec as P


def listed_mask(tile_lists, part_index, block_index):
    block_table = lax.dynamic_index_in_dim(tile_lists, part_index, 1, keepdims=False)
    listed_row = lax.dynamic_index_in_dim(block_table, block_index, 1, keepdims=False)
    block_count = tile_lists.shape[3]
    block_ids = jnp.arange(block_count, dtype=jnp.int32)
    matches = listed_row[:, :, None] == block_ids[None, None, :]
    return jnp.sum(matches.astype(jnp.float32), axis=1)


def masked_rows(integrals, listed_now):
    aux_count, block_size, orbitals = integrals.shape
    block_count = orbitals // block_size
    viewed = integrals.reshape(aux_count, block_size, block_count, block_size)
    masked = viewed[None] * listed_now[:, None, None, :, None]
    return masked.reshape(listed_now.shape[0], aux_count * block_size, orbitals)


def make_adder(masked, density_rows):
    return jnp.einsum("tar,trl->tal", masked, density_rows, precision=lax.Precision.HIGHEST)


def make_applier(column_data, density_rows):
    return jnp.einsum("tsk,takl->tasl", density_rows, column_data, precision=lax.Precision.HIGHEST)


def outgoing(product, listed_now, aux_count, block_size, block_count, split_count):
    time_count = product.shape[0]
    aux_share = aux_count // split_count
    pruned = product.reshape(time_count, aux_count, block_size, block_count, block_size)
    pruned = pruned * listed_now[:, None, None, :, None]
    split_view = pruned.reshape(
        time_count, split_count, aux_share, block_size, block_count, block_size
    )
    ordered = split_view.transpose(4, 1, 0, 2, 3, 5)
    return ordered.reshape(block_count * split_count, time_count, aux_share, block_size, block_size)


def make_arrange(block_count, split_count):

    def arrange(received):
        unit_count, time_count, item_count, row_count, col_count = received.shape
        grouped = received.reshape(
            block_count, split_count, time_count, item_count, row_count, col_count
        )
        reordered = grouped.transpose(2, 1, 3, 0, 4, 5)
        return reordered.reshape(
            time_count, split_count, item_count, block_count * row_count, col_count
        )

    return arrange


def local(three_center, tile_lists, occ_density, vir_density):
    aux_count = three_center.shape[0]
    block_size = three_center.shape[2]
    orbitals = three_center.shape[3]
    block_count = orbitals // block_size
    owners = lax.axis_size("orb")
    split_count = owners // block_count
    owner_unit = lax.axis_index("orb")
    block_index = owner_unit // split_count
    part_index = owner_unit % split_count
    listed = listed_mask(tile_lists, part_index, block_index)
    integrals = three_center[:, 0]
    arrange = make_arrange(block_count, split_count)
    occ_cols, vir_cols = (
        lax.all_gather(occ_density, "aux", axis=2, tiled=True),
        lax.all_gather(vir_density, "aux", axis=2, tiled=True),
    )
    results = []
    for moment in range(occ_cols.shape[0]):
        listed_now = listed[moment : moment + 1]
        masked = masked_rows(integrals, listed_now)
        product = make_adder(
            masked, lax.all_gather(occ_cols[moment : moment + 1], "orb", axis=1, tiled=True)
        )
        sending = outgoing(product, listed_now, aux_count, block_size, block_count, split_count)
        column_data = arrange(
            lax.all_to_all(sending, "orb", split_axis=0, concat_axis=0, tiled=True)
        )
        column_data = column_data.reshape(1, aux_count, orbitals, block_size)
        results.append(
            make_applier(
                column_data,
                lax.all_gather(vir_cols[moment : moment + 1], "orb", axis=1, tiled=True),
            )
        )
    coupled = jnp.concatenate(results, axis=0)
    return coupled[:, :, None]


def solution(mesh):
    in_specs = (
        P("aux", "orb", None, None),
        P(None, "aux", None, None),
        P(None, "orb", "aux"),
        P(None, "orb", "aux"),
    )
    out_specs = P(None, "aux", "orb", None, None)
    return jax.shard_map(local, mesh=mesh, in_specs=in_specs, out_specs=out_specs, check_vma=False)
```

profile of v0, /device:TPU:2, one launch (start us, length us, event | category | flops | bytes accessed | tf_op | source)
XLA Modules:
  0.0 402.3 jit_solution(4999827515869615526)
XLA Ops:
  6.5 0.0 copy-start
  6.5 0.0 all-gather.9.cloned.1.call-start
  6.5 13.2 %all_gather.18 = f32[2,32,1024]{2,1,0:T(8,128)S(1)} all-gather(f32[2,32,128]{2,1,0:T(8,128)} %param.6), channel_id=1, replica_groups=mesh['aux'=8,'orb'=32] {'aux'}, dimensions={2}, use_global_device_ids=true | all-gather | bytes 294912 | tf_op jit(solution)/shard_map/all_gather | solution.py:73
  19.8 0.7 fusion.23
  20.5 0.0 all-gather.9.cloned.1.call-update
  20.5 0.0 all-gather.5.cloned.1.call-start
  20.6 0.7 all-gather.5.cloned.1.call-update
  21.3 0.0 all-gather.7.cloned.1.call-start
  21.3 13.1 %all_gather.20 = f32[2,32,1024]{2,1,0:T(8,128)S(1)} all-gather(f32[2,32,128]{2,1,0:T(8,128)} %param.7), channel_id=1, replica_groups=mesh['aux'=8,'orb'=32] {'aux'}, dimensions={2}, use_global_device_ids=true | all-gather | bytes 294912 | tf_op jit(solution)/shard_map/all_gather | solution.py:74
  34.4 0.7 fusion.22
  35.1 0.0 all-gather.7.cloned.1.call-update
  35.1 0.0 copy-done
  35.2 0.1 convert_reduce_fusion
  35.3 0.1 broadcast_bitcast_fusion
  35.3 69.8 %all-gather.9.cloned.1.call-done = f32[1,1024,1024]{2,1,0:T(8,128)} async-done(((f32[1,32,1024]{2,1,0:T(8,128)}), f32[1,1024,1024]{2,1,0:T(8,128)}) %all-gather.9.cloned.1.call-update) | async-done | bytes 4194320 | tf_op jit(solution)/shard_map/all_gather | solution.py:81
  105.1 5.3 %copy.28 = f32[1024,1024]{1,0:T(8,128)} copy(f32[1024,1024]{0,1:T(8,128)} %bitcast.95) | data formatting | bytes 8388608 | tf_op jit(solution)/shard_map/tar,trl->tal/dot_general | solution.py:25
  110.4 9.4 %multiply_bitcast_fusion = f32[8,4,1,1,128,128]{5,4,0,1,3,2:T(8,128)S(1)} fusion(f32[8,128,1024,1]{2,1,0,3:T(8,128)} %bitcast.97, f32[4,1,128,1024]{3,2,1,0:T(8,128)} %param.4, f32[8]{0:T(128)S(1)} %get-tuple-element.10, f32[1024]{0:T(1024)S(1)} %get-tuple-element.11), kind=kOutput, calls=%fused_computation.9 | convolution fusion | flops 6443499520 | bytes 8392736 | tf_op jit(solution)/shard_map/tar,trl->tal/dot_general | solution.py:25
  119.9 1.5 copy.29
  121.4 5.4 %all-to-all-start.1 = ((f32[32,1,1,128,128]{4,3,2,1,0:T(8,128)}), f32[32,1,1,128,128]{4,3,2,1,0:T(8,128)S(1)}, u32[]{:S(2)}, u32[]{:S(2)}) async-start(f32[32,1,1,128,128]{4,3,2,1,0:T(8,128)} %bitcast.92), calls=%async_computation.1 | async-start | bytes 4194304 | tf_op jit(solution)/shard_map/all_to_all | solution.py:85
  126.7 0.0 all-gather.11.cloned.1.call-start
  126.8 0.5 all-gather.11.cloned.1.call-update
  127.3 72.3 %all-gather.5.cloned.1.call-done = f32[1,1024,1024]{2,1,0:T(8,128)} async-done(((f32[1,32,1024]{2,1,0:T(8,128)}), f32[1,1024,1024]{2,1,0:T(8,128)}) %all-gather.5.cloned.1.call-update) | async-done | bytes 4194320 | tf_op jit(solution)/shard_map/all_gather | solution.py:81
  199.7 5.3 %copy.24 = f32[1024,1024]{1,0:T(8,128)} copy(f32[1024,1024]{0,1:T(8,128)} %bitcast.94) | data formatting | bytes 8388608 | tf_op jit(solution)/shard_map/tar,trl->tal/dot_general | solution.py:25
  205.0 9.4 %multiply_bitcast_fusion.1 = f32[8,4,1,1,128,128]{5,4,0,1,3,2:T(8,128)S(1)} fusion(f32[8,128,1024,1]{2,1,0,3:T(8,128)} %bitcast.96, f32[4,1,128,1024]{3,2,1,0:T(8,128)} %param.4, f32[8]{0:T(128)S(1)} %get-tuple-element.9, f32[1024]{0:T(1024)S(1)} %get-tuple-element.12), kind=kOutput, calls=%fused_computation.11 | convolution fusion | flops 6443499520 | bytes 8392736 | tf_op jit(solution)/shard_map/tar,trl->tal/dot_general | solution.py:25
  214.5 1.5 copy.25
  215.9 0.0 all-to-all-done.1
  215.9 7.3 %all-to-all-start = ((f32[32,1,1,128,128]{4,3,2,1,0:T(8,128)}), f32[32,1,1,128,128]{4,3,2,1,0:T(8,128)}, u32[]{:S(2)}, u32[]{:S(2)}) async-start(f32[32,1,1,128,128]{4,3,2,1,0:T(8,128)} %bitcast.93), calls=%async_computation | async-start | bytes 4194304 | tf_op jit(solution)/shard_map/all_to_all | solution.py:85
  223.3 1.8 copy.31
  225.1 2.8 reshape.106
  227.8 55.1 %all-to-all-done = f32[32,1,1,128,128]{4,3,2,1,0:T(8,128)} async-done(((f32[32,1,1,128,128]{4,3,2,1,0:T(8,128)}), f32[32,1,1,128,128]{4,3,2,1,0:T(8,128)}, u32[]{:S(2)}, u32[]{:S(2)}) %all-to-all-start) | async-done | bytes 2097184 | tf_op jit(solution)/shard_map/all_to_all | solution.py:85
  282.9 2.1 copy.27
  285.0 1.5 reshape.100
  286.5 0.0 copy-start.1
  286.5 9.8 %all-gather.7.cloned.1.call-done = f32[1,1024,1024]{2,1,0:T(8,128)} async-done(((f32[1,32,1024]{2,1,0:T(8,128)}), f32[1,1024,1024]{2,1,0:T(8,128)}) %all-gather.7.cloned.1.call-update) | async-done | bytes 4194320 | tf_op jit(solution)/shard_map/all_gather | solution.py:91
  296.3 10.3 %fusion.14 = f32[1,4,1024,128]{2,3,1,0:T(8,128)} fusion(f32[4,1024,128]{1,2,0:T(8,128)} %reshape.100, f32[1,1024,1024]{2,1,0:T(8,128)} %all-gather.7.cloned.1.call-done), kind=kOutput, calls=%fused_computation.13 | convolution fusion | flops 6442450944 | bytes 8388608 | tf_op jit(solution)/shard_map/tsk,takl->tasl/dot_general | solution.py:29
  306.6 72.4 %all-gather.11.cloned.1.call-done = f32[1,1024,1024]{2,1,0:T(8,128)} async-done(((f32[1,32,1024]{2,1,0:T(8,128)}), f32[1,1024,1024]{2,1,0:T(8,128)}) %all-gather.11.cloned.1.call-update) | async-done | bytes 4194320 | tf_op jit(solution)/shard_map/all_gather | solution.py:91
  379.0 0.0 copy-done.1
  379.0 0.0 copy-start.2
  379.0 9.2 %fusion.17 = f32[1,4,1024,128]{2,3,1,0:T(8,128)S(1)} fusion(f32[4,1024,128]{1,2,0:T(8,128)S(1)} %copy-done.1, f32[1,1024,1024]{2,1,0:T(8,128)} %all-gather.11.cloned.1.call-done), kind=kOutput, calls=%fused_computation.14 | convolution fusion | flops 6442450944 | bytes 8388608 | tf_op jit(solution)/shard_map/tsk,takl->tasl/dot_general | solution.py:29
  388.2 0.0 copy-done.2
  388.2 2.3 maximum_bitcast_fusion
  390.5 5.3 %copy.32 = f32[2,4,1,1024,128]{4,3,2,1,0:T(8,128)} copy(f32[2,4,1,1024,128]{3,4,1,0,2:T(8,128)} %maximum_bitcast_fusion) | data formatting | bytes 8388608 | tf_op jit(solution)/shard_map/broadcast_in_dim | solution.py:95
  (2 shorter events, 0.0 us)
Async XLA Ops:
  6.5 28.6 %copy-start = (s32[2,4,8,8]{3,2,1,0:T(8,128)S(1)}, s32[2,4,8,8]{3,2,1,0:T(8,128)}, u32[]{:S(2)}) copy-start(s32[2,4,8,8]{3,2,1,0:T(8,128)} %param.5) | copy-start | bytes 6148
  6.5 98.6 %all-gather.9.cloned.1.call-start = ((), (), s32[]{:S(2)}) async-start(), calls=%async_computation.4 | async-start | bytes 4325376 | tf_op jit(solution)/shard_map/all_gather | solution.py:81
  20.5 179.2 %all-gather.5.cloned.1.call-start = ((), (), s32[]{:S(2)}) async-start(), calls=%async_computation.2 | async-start | bytes 4325376 | tf_op jit(solution)/shard_map/all_gather | solution.py:81
  21.3 275.1 %all-gather.7.cloned.1.call-start = ((), (), s32[]{:S(2)}) async-start(), calls=%async_computation.3 | async-start | bytes 4325376 | tf_op jit(solution)/shard_map/all_gather | solution.py:91
  121.4 94.6 %all-to-all-start.1 = ((f32[32,1,1,128,128]{4,3,2,1,0:T(8,128)}), f32[32,1,1,128,128]{4,3,2,1,0:T(8,128)S(1)}, u32[]{:S(2)}, u32[]{:S(2)}) async-start(f32[32,1,1,128,128]{4,3,2,1,0:T(8,128)} %bitcast.92), calls=%async_computation.1 | async-start | bytes 4194304 | tf_op jit(solution)/shard_map/all_to_all | solution.py:85
  126.7 252.3 %all-gather.11.cloned.1.call-start = ((), (), s32[]{:S(2)}) async-start(), calls=%async_computation.5 | async-start | bytes 4325376 | tf_op jit(solution)/shard_map/all_gather | solution.py:91
  215.9 67.0 %all-to-all-start = ((f32[32,1,1,128,128]{4,3,2,1,0:T(8,128)}), f32[32,1,1,128,128]{4,3,2,1,0:T(8,128)}, u32[]{:S(2)}, u32[]{:S(2)}) async-start(f32[32,1,1,128,128]{4,3,2,1,0:T(8,128)} %bitcast.93), calls=%async_computation | async-start | bytes 4194304 | tf_op jit(solution)/shard_map/all_to_all | solution.py:85
  286.5 92.5 %copy-start.1 = (f32[4,1024,128]{1,2,0:T(8,128)S(1)}, f32[4,1024,128]{1,2,0:T(8,128)}, u32[]{:S(2)}) copy-start(f32[4,1024,128]{1,2,0:T(8,128)} %reshape.106) | copy-start | bytes 6291460
  379.0 9.2 %copy-start.2 = (f32[1,4,1024,128]{2,3,1,0:T(8,128)S(1)}, f32[1,4,1024,128]{2,3,1,0:T(8,128)}, u32[]{:S(2)}) copy-start(f32[1,4,1024,128]{2,3,1,0:T(8,128)} %fusion.14) | copy-start | bytes 6291460
Sparse Core Ops, SparseCore 0:
  20.6 84.4 all-gather.8
  107.7 91.9 all-gather.4
  202.3 93.9 all-gather.6
  298.7 80.2 all-gather.10
where the time goes:
time: 403 us; the launch traced here: 402 us
  waiting for transfers between devices  281 us (70%)
  matrix products  38.4 us (10%)
  local copies, waits for them, and re-layouts  28.7 us (7%)
  blocking collectives  26.3 us (7%)
  between operations  13.2 us (3%)
  starting transfers between devices  12.8 us (3%)
    all_gather x2, waiting for transfers between devices, local(): lax.all_gather(occ_cols[moment:moment + 1], 'orb', axis=1, tiled=True)  142 us
    all_gather x2, waiting for transfers between devices, local(): lax.all_gather(vir_cols[moment:moment + 1], 'orb', axis=1, tiled=True)  82.2 us
    all_to_all x2, waiting for transfers between devices, local(): lax.all_to_all(sending, 'orb', split_axis=0, concat_axis=0, tiled=True)  55.1 us
    dot_general x2, matrix products, make_applier(): jnp.einsum('tsk,takl->tasl', density_rows, column_data, precision=lax.Pre...  19.5 us
    dot_general x2, matrix products, make_adder(): jnp.einsum('tar,trl->tal', masked, density_rows, precision=lax.Precision....  18.9 us
    all_gather x1, blocking collectives, local(): lax.all_gather(occ_density, 'aux', axis=2, tiled=True)  13.2 us
    all_gather x1, blocking collectives, local(): lax.all_gather(vir_density, 'aux', axis=2, tiled=True)  13.1 us
    all_to_all x2, starting transfers between devices, local(): lax.all_to_all(sending, 'orb', split_axis=0, concat_axis=0, tiled=True)  12.7 us
  transfers between devices with their start and end apart: 6, of which 5 were waited for; matrix products, arithmetic and copies ran while one was open for 13% of the time, Pallas kernels for 0%

commit v1 on v0

--- a/solution.py
+++ b/solution.py
@@ -88,7 +88,15 @@
         results.append(
             make_applier(
                 column_data,
-                lax.all_gather(vir_cols[moment : moment + 1], "orb", axis=1, tiled=True),
+                jnp.concatenate(
+                    lax.all_to_all(
+                        jnp.stack([vir_cols[moment : moment + 1]] * lax.axis_size("orb")),
+                        "orb",
+                        0,
+                        0,
+                    ),
+                    axis=1,
+                ),
             )
         )
     coupled = jnp.concatenate(results, axis=0)

time: 403 us -> 457 us (1.13)
  blocking collectives: 26.3 us -> 82.2 us
  waiting for transfers between devices: 281 us -> 257 us
  starting transfers between devices: 12.8 us -> 29 us
  local copies, waits for them, and re-layouts: 28.7 us -> 33.3 us
    all_gather x2 -> x0, waiting for transfers between devices: 82.2 us -> none  [local(): lax.all_gather(vir_cols[moment:moment + 1], 'orb', axis=1, tiled=True)]
    all_to_all x0 -> x2, waiting for transfers between devices: none -> 74 us  [local(): lax.all_to_all(jnp.stack([vir_cols[moment:moment + 1]] * lax.axis_size('o...]
    all_to_all x0 -> x1, blocking collectives: none -> 55.9 us  [local(): lax.all_to_all(sending, 'orb', split_axis=0, concat_axis=0, tiled=True)]
    all_to_all x2 -> x1, waiting for transfers between devices: 55.1 us -> 0.01 us  [local(): lax.all_to_all(sending, 'orb', split_axis=0, concat_axis=0, tiled=True)]
    all_gather x2, waiting for transfers between devices: 142 us -> 182 us  [local(): lax.all_gather(occ_cols[moment:moment + 1], 'orb', axis=1, tiled=True)]
    all_to_all x0 -> x2, starting transfers between devices: none -> 17.5 us  [local(): lax.all_to_all(jnp.stack([vir_cols[moment:moment + 1]] * lax.axis_size('o...]
    another operation x2 -> x4, local copies, waits for them, and re-layouts: 4.26 us -> 9.67 us  [the longest x2 5.03 us: local(): jnp.stack([vir_cols[moment:moment + 1]] * lax.axis_size('orb'))]
    all_to_all x2 -> x1, starting transfers between devices: 12.7 us -> 11.4 us  [local(): lax.all_to_all(sending, 'orb', split_axis=0, concat_axis=0, tiled=True)]
  transfers between devices with their start and end apart: 6 -> 5, of which waited for: 5 -> 3; matrix products, arithmetic and copies ran while one was open for 13% -> 12% of each run, Pallas kernels for 0% -> 0%
where the time goes in v1:
time: 457 us; the launch traced here: 455 us
  waiting for transfers between devices  257 us (56%)
  blocking collectives  82.2 us (18%)
  matrix products  37.8 us (8%)
  local copies, waits for them, and re-layouts  33.3 us (7%)
  starting transfers between devices  29 us (6%)
  between operations  13.5 us (3%)
    all_gather x2, waiting for transfers between devices, local(): lax.all_gather(occ_cols[moment:moment + 1], 'orb', axis=1, tiled=True)  182 us
    all_to_all x2, waiting for transfers between devices, local(): lax.all_to_all(jnp.stack([vir_cols[moment:moment + 1]] * lax.axis_size('o...  74 us
    all_to_all x1, blocking collectives, local(): lax.all_to_all(sending, 'orb', split_axis=0, concat_axis=0, tiled=True)  55.9 us
    dot_general x2, matrix products, make_applier(): jnp.einsum('tsk,takl->tasl', density_rows, column_data, precision=lax.Pre...  19.5 us
    dot_general x2, matrix products, make_adder(): jnp.einsum('tar,trl->tal', masked, density_rows, precision=lax.Precision....  18.2 us
    all_to_all x2, starting transfers between devices, local(): lax.all_to_all(jnp.stack([vir_cols[moment:moment + 1]] * lax.axis_size('o...  17.5 us
    all_gather x1, blocking collectives, local(): lax.all_gather(occ_density, 'aux', axis=2, tiled=True)  13.2 us
    all_gather x1, blocking collectives, local(): lax.all_gather(vir_density, 'aux', axis=2, tiled=True)  13.1 us
  transfers between devices with their start and end apart: 5, of which 3 were waited for; matrix products, arithmetic and copies ran while one was open for 12% of the time, Pallas kernels for 0%

profile of v1, /device:TPU:2, one launch (start us, length us, event | category | flops | bytes accessed | tf_op | source)
XLA Modules:
  0.0 455.2 jit_solution(2808208791058575336)
XLA Ops:
  6.5 0.0 copy-start
  6.5 0.0 all-gather.3.cloned.1.call-start
  6.5 13.2 %all_gather.12 = f32[2,32,1024]{2,1,0:T(8,128)S(1)} all-gather(f32[2,32,128]{2,1,0:T(8,128)} %param.6), channel_id=1, replica_groups=mesh['aux'=8,'orb'=32] {'aux'}, dimensions={2}, use_global_device_ids=true | all-gather | bytes 294912 | tf_op jit(solution)/shard_map/all_gather | solution.py:73
  19.8 0.7 fusion.12
  20.5 0.0 all-gather.3.cloned.1.call-update
  20.5 13.1 %all_gather.14 = f32[2,32,1024]{2,1,0:T(8,128)S(1)} all-gather(f32[2,32,128]{2,1,0:T(8,128)} %param.7), channel_id=1, replica_groups=mesh['aux'=8,'orb'=32] {'aux'}, dimensions={2}, use_global_device_ids=true | all-gather | bytes 294912 | tf_op jit(solution)/shard_map/all_gather | solution.py:74
  33.6 2.5 stack.4
  36.1 11.6 %all-to-all-start.1 = ((f32[32,1,32,1024]{3,2,1,0:T(8,128)}), f32[32,1,32,1024]{3,2,1,0:T(8,128)}, u32[]{:S(2)}, u32[]{:S(2)}) async-start(f32[32,1,32,1024]{3,2,1,0:T(8,128)} %stack.4), calls=%async_computation.1 | async-start | bytes 8388608 | tf_op jit(solution)/shard_map/all_to_all | solution.py:92
  47.7 0.0 all-gather.5.cloned.1.call-start
  47.8 0.7 all-gather.5.cloned.1.call-update
  48.5 0.0 copy-done
  48.5 0.1 convert_reduce_fusion
  48.6 0.1 broadcast_bitcast_fusion
  48.7 107.0 %all-gather.3.cloned.1.call-done = f32[1,1024,1024]{2,1,0:T(8,128)} async-done(((f32[1,32,1024]{2,1,0:T(8,128)}), f32[1,1024,1024]{2,1,0:T(8,128)}) %all-gather.3.cloned.1.call-update) | async-done | bytes 4194320 | tf_op jit(solution)/shard_map/all_gather | solution.py:81
  155.7 0.0 copy-start.4
  155.7 5.5 %copy.24 = f32[1024,1024]{1,0:T(8,128)} copy(f32[1024,1024]{0,1:T(8,128)} %bitcast.95) | data formatting | bytes 8388608 | tf_op jit(solution)/shard_map/tar,trl->tal/dot_general | solution.py:25
  161.2 0.0 copy-done.4
  161.2 8.8 %multiply_bitcast_fusion.1 = f32[8,4,1,1,128,128]{5,4,0,1,3,2:T(8,128)S(1)} fusion(f32[8,128,1024,1]{2,1,0,3:T(8,128)} %bitcast.98, f32[4,1,128,1024]{3,2,1,0:T(8,128)S(1)} %copy-done.4, f32[8]{0:T(128)S(1)} %get-tuple-element.9, f32[1024]{0:T(1024)S(1)} %get-tuple-element.12), kind=kOutput, calls=%fused_computation.7 | convolution fusion | flops 6443499520 | bytes 8392736 | tf_op jit(solution)/shard_map/tar,trl->tal/dot_general | solution.py:25
  170.0 1.5 copy.25
  171.5 0.0 all-to-all-done.1
  171.5 11.4 %all-to-all-start = ((f32[32,1,1,128,128]{4,3,2,1,0:T(8,128)}), f32[32,1,1,128,128]{4,3,2,1,0:T(8,128)S(1)}, u32[]{:S(2)}, u32[]{:S(2)}) async-start(f32[32,1,1,128,128]{4,3,2,1,0:T(8,128)} %bitcast.92), calls=%async_computation | async-start | bytes 4194304 | tf_op jit(solution)/shard_map/all_to_all | solution.py:85
  182.9 75.4 %all-gather.5.cloned.1.call-done = f32[1,1024,1024]{2,1,0:T(8,128)} async-done(((f32[1,32,1024]{2,1,0:T(8,128)}), f32[1,1024,1024]{2,1,0:T(8,128)}) %all-gather.5.cloned.1.call-update) | async-done | bytes 4194320 | tf_op jit(solution)/shard_map/all_gather | solution.py:81
  258.3 5.3 %copy.28 = f32[1024,1024]{1,0:T(8,128)} copy(f32[1024,1024]{0,1:T(8,128)} %bitcast.96) | data formatting | bytes 8388608 | tf_op jit(solution)/shard_map/tar,trl->tal/dot_general | solution.py:25
  263.7 9.4 %multiply_bitcast_fusion = f32[8,4,1,1,128,128]{5,4,0,1,3,2:T(8,128)S(1)} fusion(f32[8,128,1024,1]{2,1,0,3:T(8,128)} %bitcast.97, f32[4,1,128,1024]{3,2,1,0:T(8,128)} %param.4, f32[8]{0:T(128)S(1)} %get-tuple-element.10, f32[1024]{0:T(1024)S(1)} %get-tuple-element.11), kind=kOutput, calls=%fused_computation.5 | convolution fusion | flops 6443499520 | bytes 8392736 | tf_op jit(solution)/shard_map/tar,trl->tal/dot_general | solution.py:25
  273.1 1.5 copy.29
  274.6 0.0 all-to-all-done
  274.6 55.9 %all_to_all.20 = f32[32,1,1,128,128]{4,3,2,1,0:T(8,128)} all-to-all(f32[32,1,1,128,128]{4,3,2,1,0:T(8,128)} %bitcast.94), channel_id=1, replica_groups=mesh['aux'=8,'orb'=32] {'orb'}, dimensions={0} | all-to-all | bytes 4194304 | tf_op jit(solution)/shard_map/all_to_all | solution.py:85
  330.5 2.5 stack.5
  333.0 5.9 %all-to-all-start.3 = ((f32[32,1,32,1024]{3,2,1,0:T(8,128)}), f32[32,1,32,1024]{3,2,1,0:T(8,128)}, u32[]{:S(2)}, u32[]{:S(2)}) async-start(f32[32,1,32,1024]{3,2,1,0:T(8,128)} %stack.5), calls=%async_computation.3 | async-start | bytes 8388608 | tf_op jit(solution)/shard_map/all_to_all | solution.py:92
  338.9 1.8 copy.27
  340.8 0.0 copy-start.2
  340.8 2.9 reshape.110
  343.7 0.0 copy-done.2
  343.7 1.8 copy.31
  345.5 1.7 reshape.116
  347.3 10.3 %convolution_bitcast_fusion.1 = f32[1,4,1024,128]{2,3,1,0:T(8,128)} fusion(f32[4,1024,128]{1,2,0:T(8,128)} %reshape.110, f32[1024,1024,1]{1,0,2:T(8,128)} %bitcast.18), kind=kOutput, calls=%fused_computation.10 | convolution fusion | flops 6442450944 | bytes 8388608 | tf_op jit(solution)/shard_map/tsk,takl->tasl/dot_general | solution.py:29
  357.6 74.0 %all-to-all-done.3 = f32[32,1,32,1024]{3,2,1,0:T(8,128)} async-done(((f32[32,1,32,1024]{3,2,1,0:T(8,128)}), f32[32,1,32,1024]{3,2,1,0:T(8,128)}, u32[]{:S(2)}, u32[]{:S(2)}) %all-to-all-start.3) | async-done | bytes 4194336 | tf_op jit(solution)/shard_map/all_to_all | solution.py:92
  431.6 0.0 copy-start.3
  431.6 9.2 %convolution_bitcast_fusion = f32[1,4,1024,128]{2,3,1,0:T(8,128)S(1)} fusion(f32[4,1024,128]{1,2,0:T(8,128)S(1)} %reshape.116, f32[1024,1024,1]{1,0,2:T(8,128)} %bitcast.38), kind=kOutput, calls=%fused_computation.9 | convolution fusion | flops 6442450944 | bytes 8388608 | tf_op jit(solution)/shard_map/tsk,takl->tasl/dot_general | solution.py:29
  440.8 0.0 copy-done.3
  440.8 2.3 maximum_bitcast_fusion
  443.1 0.0 copy-start.1
  443.1 5.3 %copy.32 = f32[2,4,1,1024,128]{4,3,2,1,0:T(8,128)} copy(f32[2,4,1,1024,128]{3,4,1,0,2:T(8,128)} %maximum_bitcast_fusion) | data formatting | bytes 8388608 | tf_op jit(solution)/shard_map/broadcast_in_dim | solution.py:103
  448.4 0.0 copy-done.1
  (3 shorter events, 0.0 us)
Async XLA Ops:
  6.5 42.0 %copy-start = (s32[2,4,8,8]{3,2,1,0:T(8,128)S(1)}, s32[2,4,8,8]{3,2,1,0:T(8,128)}, u32[]{:S(2)}) copy-start(s32[2,4,8,8]{3,2,1,0:T(8,128)} %param.5) | copy-start | bytes 6148
  6.5 149.2 %all-gather.3.cloned.1.call-start = ((), (), s32[]{:S(2)}) async-start(), calls=%async_computation.4 | async-start | bytes 4325376 | tf_op jit(solution)/shard_map/all_gather | solution.py:81
  36.1 135.4 %all-to-all-start.1 = ((f32[32,1,32,1024]{3,2,1,0:T(8,128)}), f32[32,1,32,1024]{3,2,1,0:T(8,128)}, u32[]{:S(2)}, u32[]{:S(2)}) async-start(f32[32,1,32,1024]{3,2,1,0:T(8,128)} %stack.4), calls=%async_computation.1 | async-start | bytes 8388608 | tf_op jit(solution)/shard_map/all_to_all | solution.py:92
  47.7 210.6 %all-gather.5.cloned.1.call-start = ((), (), s32[]{:S(2)}) async-start(), calls=%async_computation.5 | async-start | bytes 4325376 | tf_op jit(solution)/shard_map/all_gather | solution.py:81
  155.7 5.5 %copy-start.4 = (f32[4,1,128,1024]{3,2,1,0:T(8,128)S(1)}, f32[4,1,128,1024]{3,2,1,0:T(8,128)}, u32[]{:S(2)}) copy-start(f32[4,1,128,1024]{3,2,1,0:T(8,128)} %param.4) | copy-start | bytes 6291460
  171.5 103.1 %all-to-all-start = ((f32[32,1,1,128,128]{4,3,2,1,0:T(8,128)}), f32[32,1,1,128,128]{4,3,2,1,0:T(8,128)S(1)}, u32[]{:S(2)}, u32[]{:S(2)}) async-start(f32[32,1,1,128,128]{4,3,2,1,0:T(8,128)} %bitcast.92), calls=%async_computation | async-start | bytes 4194304 | tf_op jit(solution)/shard_map/all_to_all | solution.py:85
  333.0 98.5 %all-to-all-start.3 = ((f32[32,1,32,1024]{3,2,1,0:T(8,128)}), f32[32,1,32,1024]{3,2,1,0:T(8,128)}, u32[]{:S(2)}, u32[]{:S(2)}) async-start(f32[32,1,32,1024]{3,2,1,0:T(8,128)} %stack.5), calls=%async_computation.3 | async-start | bytes 8388608 | tf_op jit(solution)/shard_map/all_to_all | solution.py:92
  340.8 2.9 copy-start.2
  431.6 9.2 %copy-start.3 = (f32[1,4,1024,128]{2,3,1,0:T(8,128)S(1)}, f32[1,4,1024,128]{2,3,1,0:T(8,128)}, u32[]{:S(2)}) copy-start(f32[1,4,1024,128]{2,3,1,0:T(8,128)} %convolution_bitcast_fusion.1) | copy-start | bytes 6291460
  443.1 5.4 %copy-start.1 = (s32[2,4,8,8]{3,2,1,0:T(8,128)S(1)}, s32[2,4,8,8]{3,2,1,0:T(8,128)}, u32[]{:S(2)}) copy-start(s32[2,4,8,8]{3,2,1,0:T(8,128)} %param.5) | copy-start | bytes 6148
Sparse Core Ops, SparseCore 0:
  20.6 135.0 all-gather.2
  158.3 99.9 all-gather.4
